TPU v7x, 256 devices: a whole 4x4x8 slice. The times are simulated.
256 devices in a mesh: req: 64 (over z, x, core), ffn: 4 (over y).
Axes of the slice: x: 4, y: 4, z: 8, core: 2. Of those that a mesh axis runs over, the one named last changes fastest.
Arguments:
- residual: bfloat16 [16384, 2048], P('req')
- queries: bfloat16 [16384, 4096], P('req', 'ffn')
- rotated_key_rows: bfloat16 [16384, 2048], P('req', 'ffn')
- values: bfloat16 [16384, 2048], P('req', 'ffn'), may hold values from -6 to 6
- req_start: int32 [16384], P('req'), may hold values from 0 to 16383, as said below
- head_sink_logit: float32 [32], P('ffn'), may hold values from 6 to 11
- out_proj: bfloat16 [4096, 2048], P('ffn', 'req'), may hold values from -0.25 to 0.25
- mid_gain: float32 [2048], replicated, may hold values from 0.1 to 1.9
- router_logits: float32 [16384, 8], P('req')
- routes: int32 [16384, 2], P('req'), may hold values from 0 to 63, as said below
- placement: int32 [64], replicated, may hold values from 0 to 7, as said below
- w_gate: bfloat16 [64, 2048, 3072], P('req', None, 'ffn'), as said below
- w_up: bfloat16 [64, 2048, 3072], P('req', None, 'ffn'), as said below
- w_down: bfloat16 [64, 2048, 3072], P('req', None, 'ffn'), as said below
Outputs:
- layer_out: bfloat16 [16384, 2048], P('req', 'ffn')
Inputs may be any that keep to these rules, and one draw needn't show every extreme that they name: req_start[p] is the first position of the request that holds position p; requests are runs of consecutive positions, each at most 8192 long, one is exactly 8192 long, and the last position is a request of one token. `routes`: the two entries of a token name indices that host different experts. Among the 512 entries of the tokens of one index of req, an index appears at most 10 times, and every index that hosts one certain expert appears exactly 10 times, in every such block. `placement`: every expert is hosted at one index or more. `w_gate`: rows k and m are equal where placement[k] == placement[m]. `w_up`: rows k and m are equal where placement[k] == placement[m]. `w_down`: rows k and m are equal where placement[k] == placement[m].
All inputs are finite; a program needn't handle non-finite values.
Results may differ from a plain program's by a relative error of at most 0.0075.
Values may be sent and summed in bfloat16 or wider, within the bound.
A program may use at most 128 MiB of HBM per device.

v0:
```python
import jax
import jax.numpy as jnp
from jax import lax
from jax.sharding import PartitionSpec as P

QUERY_HEADS = 32
KEY_VALUE_HEADS = 16
HEAD_SIZE = 128
EXPERTS = 8
EPS = 1e-06


def shifted(value, axis, steps):
    count = lax.axis_size(axis)
    initial, last = (max(0, -steps), min(count, count - steps))
    return lax.ppermute(value, axis, [(source, source + steps) for source in range(initial, last)])


def step_back(keys_in_block, values_in_block):
    return shifted((keys_in_block, values_in_block), "req", 1)


def per_device(
    residual,
    queries,
    rotated_key_rows,
    values,
    req_start,
    head_sink_logit,
    out_proj,
    mid_gain,
    router_logits,
    routes,
    placement,
    w_gate,
    w_up,
    w_down,
):
    tok_count = residual.shape[0]
    model_width = residual.shape[1]
    req_size = lax.axis_size("req")
    ffn_size = lax.axis_size("ffn")
    own_req = lax.axis_index("req")
    own_ffn = lax.axis_index("ffn")
    query_group_width = QUERY_HEADS // KEY_VALUE_HEADS
    kv_heads = rotated_key_rows.shape[1] // HEAD_SIZE
    quarter = model_width // ffn_size
    gate_mat = w_gate[0]
    up_mat = w_up[0]
    down_mat = w_down[0]
    shard_queries = queries.reshape(tok_count, kv_heads, query_group_width, HEAD_SIZE)
    local_keys = rotated_key_rows.reshape(tok_count, kv_heads, HEAD_SIZE)
    local_values = values.reshape(tok_count, kv_heads, HEAD_SIZE)
    win_span = min(16, req_size // 2)
    window = win_span * tok_count
    query_pos = own_req * tok_count + jnp.arange(tok_count, dtype=jnp.int32)
    logit_scale_factor = HEAD_SIZE ** (-0.5)

    def attend(carry_state, keys_in_block, values_in_block, key_first):
        running_max, row_total, weighted_value_sum = carry_state
        attention_logits = (
            jnp.einsum(
                "veck,uek->ecvu", shard_queries, keys_in_block, preferred_element_type=jnp.float32
            )
            * logit_scale_factor
        )
        key_pos = key_first + jnp.arange(keys_in_block.shape[0], dtype=jnp.int32)
        visible = (
            (key_pos[None, :] >= req_start[:, None])
            & (key_pos[None, :] <= query_pos[:, None])
            & (query_pos[:, None] - key_pos[None, :] < window)
        )
        attention_logits = jnp.where(visible[None, None], attention_logits, -jnp.inf)
        new_max = jnp.maximum(running_max, jnp.max(attention_logits, axis=-1))
        probs = jnp.exp(attention_logits - new_max[..., None])
        factor = jnp.exp(running_max - new_max)
        row_total = row_total * factor + jnp.sum(probs, axis=-1)
        weighted_value_sum = weighted_value_sum * factor[..., None] + jnp.einsum(
            "plyw,wpj->plyj",
            probs.astype(jnp.bfloat16),
            values_in_block,
            preferred_element_type=jnp.float32,
        )
        return (new_max, row_total, weighted_value_sum)

    initial_sink_logit = jnp.broadcast_to(
        head_sink_logit.reshape(kv_heads, query_group_width, 1),
        (kv_heads, query_group_width, tok_count),
    )
    carry_state = (
        initial_sink_logit,
        jnp.ones((kv_heads, query_group_width, tok_count), jnp.float32),
        jnp.zeros((kv_heads, query_group_width, tok_count, HEAD_SIZE), jnp.float32),
    )
    carry_state = attend(carry_state, local_keys, local_values, own_req * tok_count)
    pair_count = win_span // 2

    def pair_step(step_idx, loop_carry):
        folded, near_keys, near_values = loop_carry
        mid_keys, mid_values = step_back(near_keys, near_values)
        far_keys, far_values = step_back(mid_keys, mid_values)
        key_first = (own_req - 2 * step_idx - 2) * tok_count
        folded = attend(
            folded,
            jnp.concatenate([far_keys, mid_keys], 0),
            jnp.concatenate([far_values, mid_values], 0),
            key_first,
        )
        return (folded, far_keys, far_values)

    carry_state, unused_keys, unused_values = lax.fori_loop(
        0, pair_count, pair_step, (carry_state, local_keys, local_values)
    )
    running_max, row_total, weighted_value_sum = carry_state
    attended = (weighted_value_sum / row_total[..., None]).astype(jnp.bfloat16)
    flat_attended = jnp.transpose(attended, (2, 0, 1, 3)).reshape(tok_count, -1)
    proj = jnp.dot(
        flat_attended,
        lax.all_gather(out_proj, "req", axis=1, tiled=True),
        preferred_element_type=jnp.float32,
    )
    summed = lax.psum(proj.astype(jnp.bfloat16), "ffn").astype(jnp.float32)
    hidden_state = residual.astype(jnp.float32) + summed
    mean_sq = jnp.mean(hidden_state * hidden_state, axis=1, keepdims=True)
    normed = (hidden_state * lax.rsqrt(mean_sq + EPS) * mid_gain).astype(jnp.bfloat16)
    own_hidden = lax.dynamic_slice_in_dim(hidden_state, own_ffn * quarter, quarter, 1)
    capacity = 5 * tok_count // (2 * req_size)
    flat_routes = routes.reshape(-1)
    slot_iota = jnp.arange(req_size, dtype=jnp.int32)
    dest_hot = (flat_routes[:, None] == slot_iota[None, :]).astype(jnp.int32)
    slot_depth = jnp.sum((jnp.cumsum(dest_hot, axis=0) - dest_hot) * dest_hot, axis=1)
    slot_index = flat_routes * capacity + slot_depth
    row_tokens = jnp.arange(2 * tok_count, dtype=jnp.int32) // 2
    send_rows = (
        jnp.zeros((req_size * capacity, model_width), jnp.bfloat16)
        .at[slot_index]
        .set(normed[row_tokens])
    )
    send_rows = send_rows.reshape(req_size, capacity, model_width)
    arrived = lax.all_to_all(send_rows, "req", split_axis=0, concat_axis=0, tiled=True)
    flat_rows = arrived.reshape(-1, model_width)
    gate_val = jnp.dot(flat_rows, gate_mat, preferred_element_type=jnp.float32)
    up_val = jnp.dot(flat_rows, up_mat, preferred_element_type=jnp.float32)
    activated = (jax.nn.silu(gate_val) * up_val).astype(jnp.bfloat16)
    partial_out = lax.dot_general(
        activated, down_mat, (((1,), (1,)), ((), ())), preferred_element_type=jnp.float32
    )
    partial_rows = partial_out.astype(jnp.bfloat16).reshape(
        arrived.shape[0], arrived.shape[1], model_width
    )
    returned_parts = lax.all_to_all(
        lax.all_to_all(partial_rows[None], "req", split_axis=1, concat_axis=1, tiled=True),
        "ffn",
        split_axis=3,
        concat_axis=0,
        tiled=True,
    )
    returned = jnp.sum(returned_parts.astype(jnp.float32), axis=0)
    expert_of = jnp.sum(dest_hot * placement[None, :], axis=1).reshape(tok_count, 2)
    expert_hot = (
        expert_of[:, :, None] == jnp.arange(EXPERTS, dtype=jnp.int32)[None, None, :]
    ).astype(jnp.float32)
    chosen = jnp.sum(router_logits[:, None, :] * expert_hot, axis=2)
    logit_peak = jnp.max(chosen, axis=1, keepdims=True)
    exp_logits = jnp.exp(chosen - logit_peak)
    gate_weights = exp_logits / jnp.sum(exp_logits, axis=1, keepdims=True)
    picked = returned.reshape(req_size * capacity, quarter)[slot_index].reshape(
        tok_count, 2, quarter
    )
    mixture = jnp.sum(picked * gate_weights[:, :, None], axis=1)
    return (own_hidden + mixture).astype(jnp.bfloat16)


def solution(mesh):
    in_specs = (
        P("req", None),
        P("req", "ffn"),
        P("req", "ffn"),
        P("req", "ffn"),
        P("req"),
        P("ffn"),
        P("ffn", "req"),
        P(),
        P("req", None),
        P("req", None),
        P(),
        P("req", None, "ffn"),
        P("req", None, "ffn"),
        P("req", None, "ffn"),
    )
    out_specs = P("req", "ffn")
    return jax.shard_map(
        per_device, mesh=mesh, in_specs=in_specs, out_specs=out_specs, check_vma=False
    )
```

profile of v0, /device:TPU:32, one launch (start us, length us, event | category | flops | bytes accessed | tf_op | source)
XLA Modules:
  0.0 686.9 jit_solution(4302674995303318617)
XLA Ops:
  22.4 3.3 convolution_add_fusion
  25.7 217.4 %while.24 = (s32[]{:T(128)}, f32[4,2,256]{2,1,0:T(2,128)S(1)}, f32[4,2,256]{2,1,0:T(2,128)S(1)}, f32[4,2,256,128]{3,2,1,0:T(8,128)}, bf16[256,4,128]{2,0,1:T(8,1...) while((s32[]{:T(128)}, f32[4,2,256]{2,1,0:T(2,128)S(1)}, ...), condition=%wide.region_5.6_spmd.clone, body=%wide.region_2.5_spmd.clone.sunk | while | flops 551817984 | bytes 30547376 | solution.py:111
  27.6 3.5 collective-permute-start.2
  31.1 4.8 collective-permute-done
  41.2 5.1 collective-permute-done.1
  49.6 2.6 fusion.70
  57.1 6.0 collective-permute-done
  69.4 5.7 collective-permute-done.1
  80.2 2.6 fusion.70
  87.7 6.0 collective-permute-done
  98.5 5.3 collective-permute-done.1
  114.2 6.0 collective-permute-done
  125.0 5.3 collective-permute-done.1
  133.4 2.5 fusion.70
  140.8 6.0 collective-permute-done
  151.5 5.3 collective-permute-done.1
  159.9 2.5 fusion.70
  167.3 6.0 collective-permute-done
  178.1 5.3 collective-permute-done.1
  186.5 2.5 fusion.70
  193.9 6.0 collective-permute-done
  204.6 5.3 collective-permute-done.1
  213.0 2.5 fusion.70
  220.4 6.0 collective-permute-done
  231.2 5.3 collective-permute-done.1
  243.1 2.5 copy.111
  247.8 4.7 convolution_convert_fusion.1
  254.9 69.6 %all-reduce.2.cloned.1.call-done = bf16[256,2048]{1,0:T(8,128)(2,1)} async-done(((bf16[256,2048]{1,0:T(8,128)(2,1)}), bf16[256,2048]{1,0:T(8,128)(2,1)}) %all-reduce.2.cloned.1.call-update) | async-done | bytes 1048592 | tf_op jit(solution)/shard_map/psum | solution.py:122
  324.5 3.4 convert_add_fusion
  329.4 11.3 %scatter_custom_fusion = bf16[640,2048]{1,0:T(8,128)(2,1)} fusion(s32[512]{0:T(512)S(1)} %bitcast.136, bf16[256,2048]{1,0:T(8,128)(2,1)} %multiply_convert_fusion, s32[1024]{0:T(1024)S(1)} %pad_clamp_fusion.1, bf16[]{:T(256)} %constant.128.clone.1), kind=kCustom, calls=%fused_computation.40 | custom fusion | bytes 2621952 | tf_op jit(solution)/shard_map/scatter | solution.py:137
  340.7 5.4 reshape.364
  346.1 106.1 %all_to_all.19 = bf16[64,10,2048]{2,1,0:T(8,128)(2,1)} all-to-all(bf16[64,10,2048]{2,1,0:T(8,128)(2,1)} %reshape.364), channel_id=1, replica_groups=mesh['req'=64,'ffn'=4] {'req'}, dimensions={0} | all-to-all | bytes 5242880 | tf_op jit(solution)/shard_map/all_to_all | solution.py:140
  452.2 5.5 reshape.365
  457.7 6.2 fusion.27
  463.9 9.7 %convolution_convert_fusion = bf16[640,2048]{1,0:T(8,128)(2,1)} fusion(bf16[1,2048,768]{2,1,0:T(8,128)(2,1)S(1)} %copy-done, f32[640,768]{1,0:T(8,128)} %fusion.27, bf16[640,2048]{1,0:T(8,128)(2,1)} %reshape.365, bf16[1,2048,768]{2,1,0:T(8,128)(2,1)} %param.28), kind=kOutput, calls=%fused_computation.32 | convolution fusion | flops 4030791680 | bytes 13500416 | tf_op jit(solution)/shard_map/dot_general | solution.py:145
  473.6 5.4 broadcast_in_dim_reshape.2
  478.9 101.8 %all_to_all.20 = bf16[1,64,10,2048]{3,2,0,1:T(8,128)(2,1)} all-to-all(bf16[1,64,10,2048]{3,2,0,1:T(8,128)(2,1)} %bitcast.121), channel_id=1, replica_groups=mesh['req'=64,'ffn'=4] {'req'}, dimensions={1} | all-to-all | bytes 5242880 | tf_op jit(solution)/shard_map/all_to_all | solution.py:152
  580.8 14.3 %copy.117 = bf16[1,64,10,2048]{1,2,0,3:T(8,128)(2,1)} copy(bf16[1,64,10,2048]{3,2,0,1:T(8,128)(2,1)} %all_to_all.20) | data formatting | bytes 5242880 | tf_op jit(solution)/shard_map/all_to_all | solution.py:152
  595.1 7.5 %reshape.404 = bf16[4,2,163840]{2,1,0:T(2,128)(2,1)} reshape(bf16[2048,1,10,64]{3,2,1,0:T(8,128)(2,1)} %bitcast.119) | data formatting | bytes 5242880
  602.6 4.3 all-to-all-start.2
  607.4 31.6 %all-to-all-done.2 = bf16[4,2,163840]{2,1,0:T(2,128)(2,1)S(1)} async-done(((bf16[4,2,163840]{2,1,0:T(2,128)(2,1)}), bf16[4,2,163840]{2,1,0:T(2,128)(2,1)S(1)}, u32[]{:S(2)}, u32[]{:S(2)}) %all-to-all-start.2) | async-done | bytes 2621472 | tf_op jit(solution)/shard_map/all_to_all | solution.py:151
  638.9 5.8 reshape.405
  644.8 7.9 %copy.118 = bf16[1,64,10,2048]{3,1,2,0:T(8,128)(2,1)S(1)} copy(bf16[1,64,10,2048]{1,2,0,3:T(8,128)(2,1)} %bitcast.120) | data formatting | bytes 5242880 | tf_op jit(solution)/shard_map/all_to_all | solution.py:151
  652.6 5.5 reshape.368
  658.1 6.8 reduce_sum.94
  668.3 4.2 gather_fusion
  672.5 2.8 reshape.367
  675.4 2.6 multiply_reduce_fusion.1
  (230 shorter events, 135.5 us)
Async XLA Ops:
  6.5 457.4 %copy-start = (bf16[1,2048,768]{2,1,0:T(8,128)(2,1)S(1)}, bf16[1,2048,768]{2,1,0:T(8,128)(2,1)}, u32[]{:S(2)}) copy-start(bf16[1,2048,768]{2,1,0:T(8,128)(2,1)} %param.29) | copy-start | bytes 9437188
  6.5 8.0 %copy-start.9 = (s32[256]{0:T(256)S(1)}, s32[256]{0:T(256)}, u32[]{:S(2)}) copy-start(s32[256]{0:T(256)} %param.20) | copy-start | bytes 3076
  6.5 241.2 %all-gather.2.cloned.1.call-start = ((), (), s32[]{:S(2)}) async-start(), calls=%async_computation.3 | async-start | bytes 4259840 | tf_op jit(solution)/shard_map/all_gather | solution.py:119
  7.3 317.2 %all-reduce.2.cloned.1.call-start = ((), (), s32[]{:S(2)}) async-start(), calls=%async_computation.4 | async-start | bytes 2097152 | tf_op jit(solution)/shard_map/psum | solution.py:122
  20.6 5.1 copy-start.7
  25.7 10.2 %collective-permute-start = (bf16[256,4,128]{2,0,1:T(8,128)(2,1)S(1)}, bf16[256,4,128]{2,0,1:T(8,128)(2,1)}, u32[]{:S(2)}, u32[]{:S(2)}) collective-permute-start(bf16[256,4,128]{2,0,1:T(8,128)(2,1)S(1)} %get-tuple-element.446), channel_id=1, source_target_pairs={{0,4},{4,8},{8,12},{12,16},{16,20},{20,24},{24,28},{28,32},{32,36}... | collective-permute-start | bytes 786440 | tf_op jit(solution)/shard_map/while/body/eval_jaxpr/ppermute | solution.py:16
  27.6 11.7 %collective-permute-start.2 = (bf16[256,4,128]{2,0,1:T(8,128)(2,1)}, bf16[256,4,128]{2,0,1:T(8,128)(2,1)}, u32[]{:S(2)}, u32[]{:S(2)}) collective-permute-start(bf16[256,4,128]{2,0,1:T(8,128)(2,1)} %get-tuple-element.447), channel_id=1, source_target_pairs={{0,4},{4,8},{8,12},{12,16},{16,20},{20,24},{24,28},{28,32},{32,36}... | collective-permute-start | bytes 786440 | tf_op jit(solution)/shard_map/while/body/eval_jaxpr/ppermute | solution.py:16
  35.9 10.4 %collective-permute-start.1 = (bf16[256,4,128]{2,0,1:T(8,128)(2,1)}, bf16[256,4,128]{2,0,1:T(8,128)(2,1)S(1)}, u32[]{:S(2)}, u32[]{:S(2)}) collective-permute-start(bf16[256,4,128]{2,0,1:T(8,128)(2,1)} %collective-permute-done), channel_id=1, source_target_pairs={{0,4},{4,8},{8,12},{12,16},{16,20},{20,24},{24,28},{28,32},{32,36}... | collective-permute-start | bytes 786440 | tf_op jit(solution)/shard_map/while/body/eval_jaxpr/ppermute | solution.py:16
  39.3 10.3 %collective-permute-start.3 = (bf16[256,4,128]{2,0,1:T(8,128)(2,1)}, bf16[256,4,128]{2,0,1:T(8,128)(2,1)S(1)}, u32[]{:S(2)}, u32[]{:S(2)}) collective-permute-start(bf16[256,4,128]{2,0,1:T(8,128)(2,1)} %collective-permute-done.2), channel_id=1, source_target_pairs={{0,4},{4,8},{8,12},{12,16},{16,20},{20,24},{24,28},{28,32},{32,36}... | collective-permute-start | bytes 786440 | tf_op jit(solution)/shard_map/while/body/eval_jaxpr/ppermute | solution.py:16
  53.3 9.9 %collective-permute-start = (bf16[256,4,128]{2,0,1:T(8,128)(2,1)S(1)}, bf16[256,4,128]{2,0,1:T(8,128)(2,1)}, u32[]{:S(2)}, u32[]{:S(2)}) collective-permute-start(bf16[256,4,128]{2,0,1:T(8,128)(2,1)S(1)} %get-tuple-element.446), channel_id=1, source_target_pairs={{0,4},{4,8},{8,12},{12,16},{16,20},{20,24},{24,28},{28,32},{32,36}... | collective-permute-start | bytes 786440 | tf_op jit(solution)/shard_map/while/body/eval_jaxpr/ppermute | solution.py:16
  55.2 12.3 %collective-permute-start.2 = (bf16[256,4,128]{2,0,1:T(8,128)(2,1)}, bf16[256,4,128]{2,0,1:T(8,128)(2,1)}, u32[]{:S(2)}, u32[]{:S(2)}) collective-permute-start(bf16[256,4,128]{2,0,1:T(8,128)(2,1)} %get-tuple-element.447), channel_id=1, source_target_pairs={{0,4},{4,8},{8,12},{12,16},{16,20},{20,24},{24,28},{28,32},{32,36}... | collective-permute-start | bytes 786440 | tf_op jit(solution)/shard_map/while/body/eval_jaxpr/ppermute | solution.py:16
  63.2 11.9 %collective-permute-start.1 = (bf16[256,4,128]{2,0,1:T(8,128)(2,1)}, bf16[256,4,128]{2,0,1:T(8,128)(2,1)S(1)}, u32[]{:S(2)}, u32[]{:S(2)}) collective-permute-start(bf16[256,4,128]{2,0,1:T(8,128)(2,1)} %collective-permute-done), channel_id=1, source_target_pairs={{0,4},{4,8},{8,12},{12,16},{16,20},{20,24},{24,28},{28,32},{32,36}... | collective-permute-start | bytes 786440 | tf_op jit(solution)/shard_map/while/body/eval_jaxpr/ppermute | solution.py:16
  67.5 12.7 %collective-permute-start.3 = (bf16[256,4,128]{2,0,1:T(8,128)(2,1)}, bf16[256,4,128]{2,0,1:T(8,128)(2,1)S(1)}, u32[]{:S(2)}, u32[]{:S(2)}) collective-permute-start(bf16[256,4,128]{2,0,1:T(8,128)(2,1)} %collective-permute-done.2), channel_id=1, source_target_pairs={{0,4},{4,8},{8,12},{12,16},{16,20},{20,24},{24,28},{28,32},{32,36}... | collective-permute-start | bytes 786440 | tf_op jit(solution)/shard_map/while/body/eval_jaxpr/ppermute | solution.py:16
  77.0 3.2 copy-start.5
  83.8 9.9 %collective-permute-start = (bf16[256,4,128]{2,0,1:T(8,128)(2,1)S(1)}, bf16[256,4,128]{2,0,1:T(8,128)(2,1)}, u32[]{:S(2)}, u32[]{:S(2)}) collective-permute-start(bf16[256,4,128]{2,0,1:T(8,128)(2,1)S(1)} %get-tuple-element.446), channel_id=1, source_target_pairs={{0,4},{4,8},{8,12},{12,16},{16,20},{20,24},{24,28},{28,32},{32,36}... | collective-permute-start | bytes 786440 | tf_op jit(solution)/shard_map/while/body/eval_jaxpr/ppermute | solution.py:16
  85.7 10.8 %collective-permute-start.2 = (bf16[256,4,128]{2,0,1:T(8,128)(2,1)}, bf16[256,4,128]{2,0,1:T(8,128)(2,1)}, u32[]{:S(2)}, u32[]{:S(2)}) collective-permute-start(bf16[256,4,128]{2,0,1:T(8,128)(2,1)} %get-tuple-element.447), channel_id=1, source_target_pairs={{0,4},{4,8},{8,12},{12,16},{16,20},{20,24},{24,28},{28,32},{32,36}... | collective-permute-start | bytes 786440 | tf_op jit(solution)/shard_map/while/body/eval_jaxpr/ppermute | solution.py:16
  93.7 10.0 %collective-permute-start.1 = (bf16[256,4,128]{2,0,1:T(8,128)(2,1)}, bf16[256,4,128]{2,0,1:T(8,128)(2,1)S(1)}, u32[]{:S(2)}, u32[]{:S(2)}) collective-permute-start(bf16[256,4,128]{2,0,1:T(8,128)(2,1)} %collective-permute-done), channel_id=1, source_target_pairs={{0,4},{4,8},{8,12},{12,16},{16,20},{20,24},{24,28},{28,32},{32,36}... | collective-permute-start | bytes 786440 | tf_op jit(solution)/shard_map/while/body/eval_jaxpr/ppermute | solution.py:16
  96.5 10.0 %collective-permute-start.3 = (bf16[256,4,128]{2,0,1:T(8,128)(2,1)}, bf16[256,4,128]{2,0,1:T(8,128)(2,1)S(1)}, u32[]{:S(2)}, u32[]{:S(2)}) collective-permute-start(bf16[256,4,128]{2,0,1:T(8,128)(2,1)} %collective-permute-done.2), channel_id=1, source_target_pairs={{0,4},{4,8},{8,12},{12,16},{16,20},{20,24},{24,28},{28,32},{32,36}... | collective-permute-start | bytes 786440 | tf_op jit(solution)/shard_map/while/body/eval_jaxpr/ppermute | solution.py:16
  110.4 9.9 %collective-permute-start = (bf16[256,4,128]{2,0,1:T(8,128)(2,1)S(1)}, bf16[256,4,128]{2,0,1:T(8,128)(2,1)}, u32[]{:S(2)}, u32[]{:S(2)}) collective-permute-start(bf16[256,4,128]{2,0,1:T(8,128)(2,1)S(1)} %get-tuple-element.446), channel_id=1, source_target_pairs={{0,4},{4,8},{8,12},{12,16},{16,20},{20,24},{24,28},{28,32},{32,36}... | collective-permute-start | bytes 786440 | tf_op jit(solution)/shard_map/while/body/eval_jaxpr/ppermute | solution.py:16
  112.3 10.8 %collective-permute-start.2 = (bf16[256,4,128]{2,0,1:T(8,128)(2,1)}, bf16[256,4,128]{2,0,1:T(8,128)(2,1)}, u32[]{:S(2)}, u32[]{:S(2)}) collective-permute-start(bf16[256,4,128]{2,0,1:T(8,128)(2,1)} %get-tuple-element.447), channel_id=1, source_target_pairs={{0,4},{4,8},{8,12},{12,16},{16,20},{20,24},{24,28},{28,32},{32,36}... | collective-permute-start | bytes 786440 | tf_op jit(solution)/shard_map/while/body/eval_jaxpr/ppermute | solution.py:16
  120.3 10.0 %collective-permute-start.1 = (bf16[256,4,128]{2,0,1:T(8,128)(2,1)}, bf16[256,4,128]{2,0,1:T(8,128)(2,1)S(1)}, u32[]{:S(2)}, u32[]{:S(2)}) collective-permute-start(bf16[256,4,128]{2,0,1:T(8,128)(2,1)} %collective-permute-done), channel_id=1, source_target_pairs={{0,4},{4,8},{8,12},{12,16},{16,20},{20,24},{24,28},{28,32},{32,36}... | collective-permute-start | bytes 786440 | tf_op jit(solution)/shard_map/while/body/eval_jaxpr/ppermute | solution.py:16
  123.1 10.0 %collective-permute-start.3 = (bf16[256,4,128]{2,0,1:T(8,128)(2,1)}, bf16[256,4,128]{2,0,1:T(8,128)(2,1)S(1)}, u32[]{:S(2)}, u32[]{:S(2)}) collective-permute-start(bf16[256,4,128]{2,0,1:T(8,128)(2,1)} %collective-permute-done.2), channel_id=1, source_target_pairs={{0,4},{4,8},{8,12},{12,16},{16,20},{20,24},{24,28},{28,32},{32,36}... | collective-permute-start | bytes 786440 | tf_op jit(solution)/shard_map/while/body/eval_jaxpr/ppermute | solution.py:16
  136.9 9.9 %collective-permute-start = (bf16[256,4,128]{2,0,1:T(8,128)(2,1)S(1)}, bf16[256,4,128]{2,0,1:T(8,128)(2,1)}, u32[]{:S(2)}, u32[]{:S(2)}) collective-permute-start(bf16[256,4,128]{2,0,1:T(8,128)(2,1)S(1)} %get-tuple-element.446), channel_id=1, source_target_pairs={{0,4},{4,8},{8,12},{12,16},{16,20},{20,24},{24,28},{28,32},{32,36}... | collective-permute-start | bytes 786440 | tf_op jit(solution)/shard_map/while/body/eval_jaxpr/ppermute | solution.py:16
  138.8 10.8 %collective-permute-start.2 = (bf16[256,4,128]{2,0,1:T(8,128)(2,1)}, bf16[256,4,128]{2,0,1:T(8,128)(2,1)}, u32[]{:S(2)}, u32[]{:S(2)}) collective-permute-start(bf16[256,4,128]{2,0,1:T(8,128)(2,1)} %get-tuple-element.447), channel_id=1, source_target_pairs={{0,4},{4,8},{8,12},{12,16},{16,20},{20,24},{24,28},{28,32},{32,36}... | collective-permute-start | bytes 786440 | tf_op jit(solution)/shard_map/while/body/eval_jaxpr/ppermute | solution.py:16
  146.8 10.0 %collective-permute-start.1 = (bf16[256,4,128]{2,0,1:T(8,128)(2,1)}, bf16[256,4,128]{2,0,1:T(8,128)(2,1)S(1)}, u32[]{:S(2)}, u32[]{:S(2)}) collective-permute-start(bf16[256,4,128]{2,0,1:T(8,128)(2,1)} %collective-permute-done), channel_id=1, source_target_pairs={{0,4},{4,8},{8,12},{12,16},{16,20},{20,24},{24,28},{28,32},{32,36}... | collective-permute-start | bytes 786440 | tf_op jit(solution)/shard_map/while/body/eval_jaxpr/ppermute | solution.py:16
  149.6 10.0 %collective-permute-start.3 = (bf16[256,4,128]{2,0,1:T(8,128)(2,1)}, bf16[256,4,128]{2,0,1:T(8,128)(2,1)S(1)}, u32[]{:S(2)}, u32[]{:S(2)}) collective-permute-start(bf16[256,4,128]{2,0,1:T(8,128)(2,1)} %collective-permute-done.2), channel_id=1, source_target_pairs={{0,4},{4,8},{8,12},{12,16},{16,20},{20,24},{24,28},{28,32},{32,36}... | collective-permute-start | bytes 786440 | tf_op jit(solution)/shard_map/while/body/eval_jaxpr/ppermute | solution.py:16
  159.6 2.8 copy-start.8
  163.5 9.9 %collective-permute-start = (bf16[256,4,128]{2,0,1:T(8,128)(2,1)S(1)}, bf16[256,4,128]{2,0,1:T(8,128)(2,1)}, u32[]{:S(2)}, u32[]{:S(2)}) collective-permute-start(bf16[256,4,128]{2,0,1:T(8,128)(2,1)S(1)} %get-tuple-element.446), channel_id=1, source_target_pairs={{0,4},{4,8},{8,12},{12,16},{16,20},{20,24},{24,28},{28,32},{32,36}... | collective-permute-start | bytes 786440 | tf_op jit(solution)/shard_map/while/body/eval_jaxpr/ppermute | solution.py:16
  165.4 10.8 %collective-permute-start.2 = (bf16[256,4,128]{2,0,1:T(8,128)(2,1)}, bf16[256,4,128]{2,0,1:T(8,128)(2,1)}, u32[]{:S(2)}, u32[]{:S(2)}) collective-permute-start(bf16[256,4,128]{2,0,1:T(8,128)(2,1)} %get-tuple-element.447), channel_id=1, source_target_pairs={{0,4},{4,8},{8,12},{12,16},{16,20},{20,24},{24,28},{28,32},{32,36}... | collective-permute-start | bytes 786440 | tf_op jit(solution)/shard_map/while/body/eval_jaxpr/ppermute | solution.py:16
  173.4 10.0 %collective-permute-start.1 = (bf16[256,4,128]{2,0,1:T(8,128)(2,1)}, bf16[256,4,128]{2,0,1:T(8,128)(2,1)S(1)}, u32[]{:S(2)}, u32[]{:S(2)}) collective-permute-start(bf16[256,4,128]{2,0,1:T(8,128)(2,1)} %collective-permute-done), channel_id=1, source_target_pairs={{0,4},{4,8},{8,12},{12,16},{16,20},{20,24},{24,28},{28,32},{32,36}... | collective-permute-start | bytes 786440 | tf_op jit(solution)/shard_map/while/body/eval_jaxpr/ppermute | solution.py:16
  176.2 10.0 %collective-permute-start.3 = (bf16[256,4,128]{2,0,1:T(8,128)(2,1)}, bf16[256,4,128]{2,0,1:T(8,128)(2,1)S(1)}, u32[]{:S(2)}, u32[]{:S(2)}) collective-permute-start(bf16[256,4,128]{2,0,1:T(8,128)(2,1)} %collective-permute-done.2), channel_id=1, source_target_pairs={{0,4},{4,8},{8,12},{12,16},{16,20},{20,24},{24,28},{28,32},{32,36}... | collective-permute-start | bytes 786440 | tf_op jit(solution)/shard_map/while/body/eval_jaxpr/ppermute | solution.py:16
  186.2 2.8 copy-start.8
  190.0 9.9 %collective-permute-start = (bf16[256,4,128]{2,0,1:T(8,128)(2,1)S(1)}, bf16[256,4,128]{2,0,1:T(8,128)(2,1)}, u32[]{:S(2)}, u32[]{:S(2)}) collective-permute-start(bf16[256,4,128]{2,0,1:T(8,128)(2,1)S(1)} %get-tuple-element.446), channel_id=1, source_target_pairs={{0,4},{4,8},{8,12},{12,16},{16,20},{20,24},{24,28},{28,32},{32,36}... | collective-permute-start | bytes 786440 | tf_op jit(solution)/shard_map/while/body/eval_jaxpr/ppermute | solution.py:16
  191.9 10.8 %collective-permute-start.2 = (bf16[256,4,128]{2,0,1:T(8,128)(2,1)}, bf16[256,4,128]{2,0,1:T(8,128)(2,1)}, u32[]{:S(2)}, u32[]{:S(2)}) collective-permute-start(bf16[256,4,128]{2,0,1:T(8,128)(2,1)} %get-tuple-element.447), channel_id=1, source_target_pairs={{0,4},{4,8},{8,12},{12,16},{16,20},{20,24},{24,28},{28,32},{32,36}... | collective-permute-start | bytes 786440 | tf_op jit(solution)/shard_map/while/body/eval_jaxpr/ppermute | solution.py:16
  199.9 10.0 %collective-permute-start.1 = (bf16[256,4,128]{2,0,1:T(8,128)(2,1)}, bf16[256,4,128]{2,0,1:T(8,128)(2,1)S(1)}, u32[]{:S(2)}, u32[]{:S(2)}) collective-permute-start(bf16[256,4,128]{2,0,1:T(8,128)(2,1)} %collective-permute-done), channel_id=1, source_target_pairs={{0,4},{4,8},{8,12},{12,16},{16,20},{20,24},{24,28},{28,32},{32,36}... | collective-permute-start | bytes 786440 | tf_op jit(solution)/shard_map/while/body/eval_jaxpr/ppermute | solution.py:16
  202.7 10.0 %collective-permute-start.3 = (bf16[256,4,128]{2,0,1:T(8,128)(2,1)}, bf16[256,4,128]{2,0,1:T(8,128)(2,1)S(1)}, u32[]{:S(2)}, u32[]{:S(2)}) collective-permute-start(bf16[256,4,128]{2,0,1:T(8,128)(2,1)} %collective-permute-done.2), channel_id=1, source_target_pairs={{0,4},{4,8},{8,12},{12,16},{16,20},{20,24},{24,28},{28,32},{32,36}... | collective-permute-start | bytes 786440 | tf_op jit(solution)/shard_map/while/body/eval_jaxpr/ppermute | solution.py:16
  216.6 9.9 %collective-permute-start = (bf16[256,4,128]{2,0,1:T(8,128)(2,1)S(1)}, bf16[256,4,128]{2,0,1:T(8,128)(2,1)}, u32[]{:S(2)}, u32[]{:S(2)}) collective-permute-start(bf16[256,4,128]{2,0,1:T(8,128)(2,1)S(1)} %get-tuple-element.446), channel_id=1, source_target_pairs={{0,4},{4,8},{8,12},{12,16},{16,20},{20,24},{24,28},{28,32},{32,36}... | collective-permute-start | bytes 786440 | tf_op jit(solution)/shard_map/while/body/eval_jaxpr/ppermute | solution.py:16
  218.5 10.8 %collective-permute-start.2 = (bf16[256,4,128]{2,0,1:T(8,128)(2,1)}, bf16[256,4,128]{2,0,1:T(8,128)(2,1)}, u32[]{:S(2)}, u32[]{:S(2)}) collective-permute-start(bf16[256,4,128]{2,0,1:T(8,128)(2,1)} %get-tuple-element.447), channel_id=1, source_target_pairs={{0,4},{4,8},{8,12},{12,16},{16,20},{20,24},{24,28},{28,32},{32,36}... | collective-permute-start | bytes 786440 | tf_op jit(solution)/shard_map/while/body/eval_jaxpr/ppermute | solution.py:16
  226.5 10.0 %collective-permute-start.1 = (bf16[256,4,128]{2,0,1:T(8,128)(2,1)}, bf16[256,4,128]{2,0,1:T(8,128)(2,1)S(1)}, u32[]{:S(2)}, u32[]{:S(2)}) collective-permute-start(bf16[256,4,128]{2,0,1:T(8,128)(2,1)} %collective-permute-done), channel_id=1, source_target_pairs={{0,4},{4,8},{8,12},{12,16},{16,20},{20,24},{24,28},{28,32},{32,36}... | collective-permute-start | bytes 786440 | tf_op jit(solution)/shard_map/while/body/eval_jaxpr/ppermute | solution.py:16
  229.3 10.0 %collective-permute-start.3 = (bf16[256,4,128]{2,0,1:T(8,128)(2,1)}, bf16[256,4,128]{2,0,1:T(8,128)(2,1)S(1)}, u32[]{:S(2)}, u32[]{:S(2)}) collective-permute-start(bf16[256,4,128]{2,0,1:T(8,128)(2,1)} %collective-permute-done.2), channel_id=1, source_target_pairs={{0,4},{4,8},{8,12},{12,16},{16,20},{20,24},{24,28},{28,32},{32,36}... | collective-permute-start | bytes 786440 | tf_op jit(solution)/shard_map/while/body/eval_jaxpr/ppermute | solution.py:16
  247.8 6.6 copy-start.11
  247.8 7.0 %copy-start.13 = (s32[64]{0:T(128)S(1)}, s32[64]{0:T(128)}, u32[]{:S(2)}) copy-start(s32[64]{0:T(128)} %param.26) | copy-start | bytes 772
  252.5 75.4 %copy-start.10 = (f32[2048]{0:T(1024)S(1)}, f32[2048]{0:T(1024)}, u32[]{:S(2)}) copy-start(f32[2048]{0:T(1024)} %param.23) | copy-start | bytes 24580
  324.5 3.4 copy-start.3
  324.5 3.4 copy-start.4
  602.6 4.5 copy-start.12
  602.6 36.3 %all-to-all-start.2 = ((bf16[4,2,163840]{2,1,0:T(2,128)(2,1)}), bf16[4,2,163840]{2,1,0:T(2,128)(2,1)S(1)}, u32[]{:S(2)}, u32[]{:S(2)}) async-start(bf16[4,2,163840]{2,1,0:T(2,128)(2,1)} %reshape.404), calls=%async_computation.2 | async-start | bytes 5242880 | tf_op jit(solution)/shard_map/all_to_all | solution.py:151
  668.3 11.5 %copy-start.1 = (bf16[1,2048,768]{2,1,0:T(8,128)(2,1)S(1)}, bf16[1,2048,768]{2,1,0:T(8,128)(2,1)}, u32[]{:S(2)}) copy-start(bf16[1,2048,768]{2,1,0:T(8,128)(2,1)} %param.29) | copy-start | bytes 9437188
  (22 other events, 34.7 us)
Sparse Core Ops, SparseCore 0:
  10.1 83.0 all-gather.1
  252.6 71.8 all-reduce.1
where the time goes:
time: 696 us; the launch traced here: 687 us
  blocking collectives  208 us (30%)
  waiting for transfers between devices  201 us (29%)
  local copies, waits for them, and re-layouts  105 us (15%)
  starting transfers between devices  67.1 us (10%)
  matrix products  60.8 us (9%)
  other arithmetic  29.8 us (4%)
  between operations  13.9 us (2%)
    all_to_all x1, blocking collectives, per_device(): lax.all_to_all(send_rows, 'req', split_axis=0, concat_axis=0, tiled=True)  106 us
    all_to_all x1, blocking collectives, per_device(): lax.all_to_all(partial_rows[None], 'req', split_axis=1, concat_axis=1, ti...  102 us
    ppermute x32, waiting for transfers between devices, shifted(): lax.ppermute(value, axis, [(source, source + steps) for source in range(i...  99.5 us
    psum x1, waiting for transfers between devices, per_device(): summed = lax.psum(proj.astype(jnp.bfloat16), 'ffn').astype(jnp.float32)  69.6 us
    ppermute x32, starting transfers between devices, shifted(): lax.ppermute(value, axis, [(source, source + steps) for source in range(i...  62.8 us
    all_to_all x1, waiting for transfers between devices, per_device(): lax.all_to_all(lax.all_to_all(partial_rows[None], 'req', split_axis=1, co...  31.6 us
    unnamed x31, local copies, waits for them, and re-layouts  25.2 us
    dot_general x9, matrix products, attend(): jnp.einsum('plyw,wpj->plyj', probs.astype(jnp.bfloat16), values_in_block,...  23.7 us
  transfers between devices with their start and end apart: 35, of which 28 were waited for; matrix products, arithmetic and copies ran while one was open for 10% of the time, Pallas kernels for 0%

commit v1 on v0

--- a/solution.py
+++ b/solution.py
@@ -2,6 +2,7 @@
 import jax.numpy as jnp
 from jax import lax
 from jax.sharding import PartitionSpec as P
+from jax.lax import all_to_all, axis_size
 
 QUERY_HEADS = 32
 KEY_VALUE_HEADS = 16
@@ -148,13 +149,9 @@
     partial_rows = partial_out.astype(jnp.bfloat16).reshape(
         arrived.shape[0], arrived.shape[1], model_width
     )
-    returned_parts = lax.all_to_all(
-        lax.all_to_all(partial_rows[None], "req", split_axis=1, concat_axis=1, tiled=True),
-        "ffn",
-        split_axis=3,
-        concat_axis=0,
-        tiled=True,
-    )
+    target = lax.all_to_all(partial_rows[None], "req", split_axis=1, concat_axis=1, tiled=True)
+    answer = all_to_all(jnp.stack(jnp.split(target, axis_size("ffn"), axis=3), axis=0), "ffn", 0, 0)
+    returned_parts = jnp.concatenate(answer, axis=0)
     returned = jnp.sum(returned_parts.astype(jnp.float32), axis=0)
     expert_of = jnp.sum(dest_hot * placement[None, :], axis=1).reshape(tok_count, 2)
     expert_hot = (

time: 696 us -> 650 us (0.934)
  local copies, waits for them, and re-layouts: 105 us -> 68.5 us
    all_to_all x2 -> x0, local copies, waits for them, and re-layouts: 22.2 us -> none  [the longest x1 14.3 us: per_device(): lax.all_to_all(partial_rows[None], 'req', split_axis=1, concat_axis=1, ti...]
    unnamed x31 -> x27, local copies, waits for them, and re-layouts: 25.2 us -> 11.9 us
  transfers between devices with their start and end apart: 35 -> 35, of which waited for: 28 -> 28; matrix products, arithmetic and copies ran while one was open for 10% -> 11% of each run, Pallas kernels for 0% -> 0%
where the time goes in v1:
time: 650 us; the launch traced here: 647 us
  blocking collectives  207 us (32%)
  waiting for transfers between devices  202 us (31%)
  local copies, waits for them, and re-layouts  68.5 us (11%)
  starting transfers between devices  67.7 us (10%)
  matrix products  60.8 us (9%)
  other arithmetic  25.8 us (4%)
  between operations  13.7 us (2%)
    all_to_all x1, blocking collectives, per_device(): lax.all_to_all(send_rows, 'req', split_axis=0, concat_axis=0, tiled=True)  106 us
    all_to_all x1, blocking collectives, per_device(): lax.all_to_all(partial_rows[None], 'req', split_axis=1, concat_axis=1, ti...  102 us
    ppermute x32, waiting for transfers between devices, shifted(): lax.ppermute(value, axis, [(source, source + steps) for source in range(i...  99.5 us
    psum x1, waiting for transfers between devices, per_device(): summed = lax.psum(proj.astype(jnp.bfloat16), 'ffn').astype(jnp.float32)  69.9 us
    ppermute x32, starting transfers between devices, shifted(): lax.ppermute(value, axis, [(source, source + steps) for source in range(i...  62.8 us
    all_to_all x1, waiting for transfers between devices, per_device(): all_to_all(jnp.stack(jnp.split(target, axis_size('ffn'), axis=3), axis=0)...  31.6 us
    dot_general x9, matrix products, attend(): jnp.einsum('plyw,wpj->plyj', probs.astype(jnp.bfloat16), values_in_block,...  23.7 us
    dot_general x9, matrix products, attend(): jnp.einsum('veck,uek->ecvu', shard_queries, keys_in_block, preferred_elem...  16.6 us
  transfers between devices with their start and end apart: 35, of which 28 were waited for; matrix products, arithmetic and copies ran while one was open for 11% of the time, Pallas kernels for 0%

profile of v1, /device:TPU:32, one launch (start us, length us, event | category | flops | bytes accessed | tf_op | source)
XLA Modules:
  0.0 646.8 jit_solution(13950032560015892701)
XLA Ops:
  22.5 3.2 convolution_add_fusion
  25.7 217.2 %while.24 = (s32[]{:T(128)}, f32[4,2,256]{2,1,0:T(2,128)S(1)}, f32[4,2,256]{2,1,0:T(2,128)S(1)}, f32[4,2,256,128]{3,2,1,0:T(8,128)}, bf16[256,4,128]{2,0,1:T(8,1...) while((s32[]{:T(128)}, f32[4,2,256]{2,1,0:T(2,128)S(1)}, ...), condition=%wide.region_5.6_spmd.clone, body=%wide.region_2.5_spmd.clone.sunk | while | flops 551817984 | bytes 30547376 | solution.py:112
  27.6 3.5 collective-permute-start.2
  31.2 4.8 collective-permute-done
  41.2 5.1 collective-permute-done.1
  49.7 2.6 fusion.70
  57.1 6.0 collective-permute-done
  69.4 5.7 collective-permute-done.1
  77.9 2.3 collective-permute-done.3
  80.2 2.6 fusion.70
  87.7 6.0 collective-permute-done
  98.4 5.3 collective-permute-done.1
  106.8 2.5 fusion.70
  114.2 6.0 collective-permute-done
  124.9 5.3 collective-permute-done.1
  133.3 2.5 fusion.70
  140.7 6.0 collective-permute-done
  151.5 5.3 collective-permute-done.1
  159.8 2.5 fusion.70
  167.2 6.0 collective-permute-done
  178.0 5.3 collective-permute-done.1
  186.4 2.5 fusion.70
  193.7 6.0 collective-permute-done
  204.5 5.3 collective-permute-done.1
  212.9 2.5 fusion.70
  220.3 6.0 collective-permute-done
  231.0 5.3 collective-permute-done.1
  239.4 2.5 fusion.70
  242.9 2.6 copy.91
  247.6 4.7 convolution_convert_fusion.1
  254.4 69.9 %all-reduce.2.cloned.1.call-done = bf16[256,2048]{1,0:T(8,128)(2,1)} async-done(((bf16[256,2048]{1,0:T(8,128)(2,1)}), bf16[256,2048]{1,0:T(8,128)(2,1)}) %all-reduce.2.cloned.1.call-update) | async-done | bytes 1048592 | tf_op jit(solution)/shard_map/psum | solution.py:123
  324.4 3.4 convert_add_fusion
  329.3 11.3 %scatter_custom_fusion = bf16[640,2048]{1,0:T(8,128)(2,1)} fusion(s32[512]{0:T(512)S(1)} %bitcast.140, bf16[256,2048]{1,0:T(8,128)(2,1)} %multiply_convert_fusion, s32[1024]{0:T(1024)S(1)} %pad_clamp_fusion.1, bf16[]{:T(256)} %constant.128.clone.1), kind=kCustom, calls=%fused_computation.42 | custom fusion | bytes 2621952 | tf_op jit(solution)/shard_map/scatter | solution.py:138
  340.6 5.4 reshape.362
  346.0 105.9 %all_to_all.15 = bf16[64,10,2048]{2,1,0:T(8,128)(2,1)} all-to-all(bf16[64,10,2048]{2,1,0:T(8,128)(2,1)} %reshape.362), channel_id=1, replica_groups=mesh['req'=64,'ffn'=4] {'req'}, dimensions={0} | all-to-all | bytes 5242880 | tf_op jit(solution)/shard_map/all_to_all | solution.py:141
  451.9 5.5 reshape.363
  457.4 6.2 fusion.27
  463.6 9.7 %convolution_convert_fusion = bf16[640,2048]{1,0:T(8,128)(2,1)} fusion(bf16[1,2048,768]{2,1,0:T(8,128)(2,1)S(1)} %copy-done, f32[640,768]{1,0:T(8,128)} %fusion.27, bf16[640,2048]{1,0:T(8,128)(2,1)} %reshape.363, bf16[1,2048,768]{2,1,0:T(8,128)(2,1)} %param.28), kind=kOutput, calls=%fused_computation.34 | convolution fusion | flops 4030791680 | bytes 13500416 | tf_op jit(solution)/shard_map/dot_general | solution.py:146
  473.3 5.4 broadcast_in_dim_reshape.2
  478.7 101.6 %all_to_all.16 = bf16[1,64,10,2048]{3,2,0,1:T(8,128)(2,1)S(1)} all-to-all(bf16[1,64,10,2048]{3,2,0,1:T(8,128)(2,1)} %bitcast.125), channel_id=1, replica_groups=mesh['req'=64,'ffn'=4] {'req'}, dimensions={1} | all-to-all | bytes 5242880 | tf_op jit(solution)/shard_map/all_to_all | solution.py:152
  581.6 3.0 copy.100
  584.6 4.9 all-to-all-start.2
  590.1 31.6 %all-to-all-done.2 = bf16[4,1,64,10,512]{4,2,3,1,0:T(8,128)(2,1)} async-done(((bf16[4,1,64,10,512]{4,2,3,1,0:T(8,128)(2,1)}), bf16[4,1,64,10,512]{4,2,3,1,0:T(8,128)(2,1)}, u32[]{:S(2)}, u32[]{:S(2)}) %all-to-all-start.2) | async-done | bytes 2621472 | tf_op jit(solution)/shard_map/all_to_all | solution.py:153
  621.7 2.3 convert_reduce_fusion
  626.2 2.5 reshape.364
  628.7 4.0 gather_fusion
  632.7 2.8 reshape.365
  635.5 2.6 multiply_reduce_fusion.1
  (227 shorter events, 127.8 us)
Async XLA Ops:
  6.5 457.1 %copy-start = (bf16[1,2048,768]{2,1,0:T(8,128)(2,1)S(1)}, bf16[1,2048,768]{2,1,0:T(8,128)(2,1)}, u32[]{:S(2)}) copy-start(bf16[1,2048,768]{2,1,0:T(8,128)(2,1)} %param.29) | copy-start | bytes 9437188
  6.5 8.0 %copy-start.8 = (s32[256]{0:T(256)S(1)}, s32[256]{0:T(256)}, u32[]{:S(2)}) copy-start(s32[256]{0:T(256)} %param.20) | copy-start | bytes 3076
  6.5 241.1 %all-gather.2.cloned.1.call-start = ((), (), s32[]{:S(2)}) async-start(), calls=%async_computation.3 | async-start | bytes 4259840 | tf_op jit(solution)/shard_map/all_gather | solution.py:120
  7.3 317.1 %all-reduce.2.cloned.1.call-start = ((), (), s32[]{:S(2)}) async-start(), calls=%async_computation.4 | async-start | bytes 2097152 | tf_op jit(solution)/shard_map/psum | solution.py:123
  20.6 5.1 copy-start.6
  25.7 10.2 %collective-permute-start = (bf16[256,4,128]{2,0,1:T(8,128)(2,1)S(1)}, bf16[256,4,128]{2,0,1:T(8,128)(2,1)}, u32[]{:S(2)}, u32[]{:S(2)}) collective-permute-start(bf16[256,4,128]{2,0,1:T(8,128)(2,1)S(1)} %get-tuple-element.439), channel_id=1, source_target_pairs={{0,4},{4,8},{8,12},{12,16},{16,20},{20,24},{24,28},{28,32},{32,36}... | collective-permute-start | bytes 786440 | tf_op jit(solution)/shard_map/while/body/eval_jaxpr/ppermute | solution.py:17
  27.6 11.7 %collective-permute-start.2 = (bf16[256,4,128]{2,0,1:T(8,128)(2,1)}, bf16[256,4,128]{2,0,1:T(8,128)(2,1)}, u32[]{:S(2)}, u32[]{:S(2)}) collective-permute-start(bf16[256,4,128]{2,0,1:T(8,128)(2,1)} %get-tuple-element.440), channel_id=1, source_target_pairs={{0,4},{4,8},{8,12},{12,16},{16,20},{20,24},{24,28},{28,32},{32,36}... | collective-permute-start | bytes 786440 | tf_op jit(solution)/shard_map/while/body/eval_jaxpr/ppermute | solution.py:17
  36.0 10.4 %collective-permute-start.1 = (bf16[256,4,128]{2,0,1:T(8,128)(2,1)}, bf16[256,4,128]{2,0,1:T(8,128)(2,1)S(1)}, u32[]{:S(2)}, u32[]{:S(2)}) collective-permute-start(bf16[256,4,128]{2,0,1:T(8,128)(2,1)} %collective-permute-done), channel_id=1, source_target_pairs={{0,4},{4,8},{8,12},{12,16},{16,20},{20,24},{24,28},{28,32},{32,36}... | collective-permute-start | bytes 786440 | tf_op jit(solution)/shard_map/while/body/eval_jaxpr/ppermute | solution.py:17
  39.3 10.3 %collective-permute-start.3 = (bf16[256,4,128]{2,0,1:T(8,128)(2,1)}, bf16[256,4,128]{2,0,1:T(8,128)(2,1)S(1)}, u32[]{:S(2)}, u32[]{:S(2)}) collective-permute-start(bf16[256,4,128]{2,0,1:T(8,128)(2,1)} %collective-permute-done.2), channel_id=1, source_target_pairs={{0,4},{4,8},{8,12},{12,16},{16,20},{20,24},{24,28},{28,32},{32,36}... | collective-permute-start | bytes 786440 | tf_op jit(solution)/shard_map/while/body/eval_jaxpr/ppermute | solution.py:17
  53.3 9.9 %collective-permute-start = (bf16[256,4,128]{2,0,1:T(8,128)(2,1)S(1)}, bf16[256,4,128]{2,0,1:T(8,128)(2,1)}, u32[]{:S(2)}, u32[]{:S(2)}) collective-permute-start(bf16[256,4,128]{2,0,1:T(8,128)(2,1)S(1)} %get-tuple-element.439), channel_id=1, source_target_pairs={{0,4},{4,8},{8,12},{12,16},{16,20},{20,24},{24,28},{28,32},{32,36}... | collective-permute-start | bytes 786440 | tf_op jit(solution)/shard_map/while/body/eval_jaxpr/ppermute | solution.py:17
  55.2 12.3 %collective-permute-start.2 = (bf16[256,4,128]{2,0,1:T(8,128)(2,1)}, bf16[256,4,128]{2,0,1:T(8,128)(2,1)}, u32[]{:S(2)}, u32[]{:S(2)}) collective-permute-start(bf16[256,4,128]{2,0,1:T(8,128)(2,1)} %get-tuple-element.440), channel_id=1, source_target_pairs={{0,4},{4,8},{8,12},{12,16},{16,20},{20,24},{24,28},{28,32},{32,36}... | collective-permute-start | bytes 786440 | tf_op jit(solution)/shard_map/while/body/eval_jaxpr/ppermute | solution.py:17
  63.2 11.9 %collective-permute-start.1 = (bf16[256,4,128]{2,0,1:T(8,128)(2,1)}, bf16[256,4,128]{2,0,1:T(8,128)(2,1)S(1)}, u32[]{:S(2)}, u32[]{:S(2)}) collective-permute-start(bf16[256,4,128]{2,0,1:T(8,128)(2,1)} %collective-permute-done), channel_id=1, source_target_pairs={{0,4},{4,8},{8,12},{12,16},{16,20},{20,24},{24,28},{28,32},{32,36}... | collective-permute-start | bytes 786440 | tf_op jit(solution)/shard_map/while/body/eval_jaxpr/ppermute | solution.py:17
  67.5 12.7 %collective-permute-start.3 = (bf16[256,4,128]{2,0,1:T(8,128)(2,1)}, bf16[256,4,128]{2,0,1:T(8,128)(2,1)S(1)}, u32[]{:S(2)}, u32[]{:S(2)}) collective-permute-start(bf16[256,4,128]{2,0,1:T(8,128)(2,1)} %collective-permute-done.2), channel_id=1, source_target_pairs={{0,4},{4,8},{8,12},{12,16},{16,20},{20,24},{24,28},{28,32},{32,36}... | collective-permute-start | bytes 786440 | tf_op jit(solution)/shard_map/while/body/eval_jaxpr/ppermute | solution.py:17
  77.0 3.2 copy-start.4
  83.8 9.9 %collective-permute-start = (bf16[256,4,128]{2,0,1:T(8,128)(2,1)S(1)}, bf16[256,4,128]{2,0,1:T(8,128)(2,1)}, u32[]{:S(2)}, u32[]{:S(2)}) collective-permute-start(bf16[256,4,128]{2,0,1:T(8,128)(2,1)S(1)} %get-tuple-element.439), channel_id=1, source_target_pairs={{0,4},{4,8},{8,12},{12,16},{16,20},{20,24},{24,28},{28,32},{32,36}... | collective-permute-start | bytes 786440 | tf_op jit(solution)/shard_map/while/body/eval_jaxpr/ppermute | solution.py:17
  85.7 10.8 %collective-permute-start.2 = (bf16[256,4,128]{2,0,1:T(8,128)(2,1)}, bf16[256,4,128]{2,0,1:T(8,128)(2,1)}, u32[]{:S(2)}, u32[]{:S(2)}) collective-permute-start(bf16[256,4,128]{2,0,1:T(8,128)(2,1)} %get-tuple-element.440), channel_id=1, source_target_pairs={{0,4},{4,8},{8,12},{12,16},{16,20},{20,24},{24,28},{28,32},{32,36}... | collective-permute-start | bytes 786440 | tf_op jit(solution)/shard_map/while/body/eval_jaxpr/ppermute | solution.py:17
  93.7 10.0 %collective-permute-start.1 = (bf16[256,4,128]{2,0,1:T(8,128)(2,1)}, bf16[256,4,128]{2,0,1:T(8,128)(2,1)S(1)}, u32[]{:S(2)}, u32[]{:S(2)}) collective-permute-start(bf16[256,4,128]{2,0,1:T(8,128)(2,1)} %collective-permute-done), channel_id=1, source_target_pairs={{0,4},{4,8},{8,12},{12,16},{16,20},{20,24},{24,28},{28,32},{32,36}... | collective-permute-start | bytes 786440 | tf_op jit(solution)/shard_map/while/body/eval_jaxpr/ppermute | solution.py:17
  96.5 10.0 %collective-permute-start.3 = (bf16[256,4,128]{2,0,1:T(8,128)(2,1)}, bf16[256,4,128]{2,0,1:T(8,128)(2,1)S(1)}, u32[]{:S(2)}, u32[]{:S(2)}) collective-permute-start(bf16[256,4,128]{2,0,1:T(8,128)(2,1)} %collective-permute-done.2), channel_id=1, source_target_pairs={{0,4},{4,8},{8,12},{12,16},{16,20},{20,24},{24,28},{28,32},{32,36}... | collective-permute-start | bytes 786440 | tf_op jit(solution)/shard_map/while/body/eval_jaxpr/ppermute | solution.py:17
  110.3 9.9 %collective-permute-start = (bf16[256,4,128]{2,0,1:T(8,128)(2,1)S(1)}, bf16[256,4,128]{2,0,1:T(8,128)(2,1)}, u32[]{:S(2)}, u32[]{:S(2)}) collective-permute-start(bf16[256,4,128]{2,0,1:T(8,128)(2,1)S(1)} %get-tuple-element.439), channel_id=1, source_target_pairs={{0,4},{4,8},{8,12},{12,16},{16,20},{20,24},{24,28},{28,32},{32,36}... | collective-permute-start | bytes 786440 | tf_op jit(solution)/shard_map/while/body/eval_jaxpr/ppermute | solution.py:17
  112.2 10.8 %collective-permute-start.2 = (bf16[256,4,128]{2,0,1:T(8,128)(2,1)}, bf16[256,4,128]{2,0,1:T(8,128)(2,1)}, u32[]{:S(2)}, u32[]{:S(2)}) collective-permute-start(bf16[256,4,128]{2,0,1:T(8,128)(2,1)} %get-tuple-element.440), channel_id=1, source_target_pairs={{0,4},{4,8},{8,12},{12,16},{16,20},{20,24},{24,28},{28,32},{32,36}... | collective-permute-start | bytes 786440 | tf_op jit(solution)/shard_map/while/body/eval_jaxpr/ppermute | solution.py:17
  120.2 10.0 %collective-permute-start.1 = (bf16[256,4,128]{2,0,1:T(8,128)(2,1)}, bf16[256,4,128]{2,0,1:T(8,128)(2,1)S(1)}, u32[]{:S(2)}, u32[]{:S(2)}) collective-permute-start(bf16[256,4,128]{2,0,1:T(8,128)(2,1)} %collective-permute-done), channel_id=1, source_target_pairs={{0,4},{4,8},{8,12},{12,16},{16,20},{20,24},{24,28},{28,32},{32,36}... | collective-permute-start | bytes 786440 | tf_op jit(solution)/shard_map/while/body/eval_jaxpr/ppermute | solution.py:17
  123.0 10.0 %collective-permute-start.3 = (bf16[256,4,128]{2,0,1:T(8,128)(2,1)}, bf16[256,4,128]{2,0,1:T(8,128)(2,1)S(1)}, u32[]{:S(2)}, u32[]{:S(2)}) collective-permute-start(bf16[256,4,128]{2,0,1:T(8,128)(2,1)} %collective-permute-done.2), channel_id=1, source_target_pairs={{0,4},{4,8},{8,12},{12,16},{16,20},{20,24},{24,28},{28,32},{32,36}... | collective-permute-start | bytes 786440 | tf_op jit(solution)/shard_map/while/body/eval_jaxpr/ppermute | solution.py:17
  133.0 2.8 copy-start.7
  136.8 9.9 %collective-permute-start = (bf16[256,4,128]{2,0,1:T(8,128)(2,1)S(1)}, bf16[256,4,128]{2,0,1:T(8,128)(2,1)}, u32[]{:S(2)}, u32[]{:S(2)}) collective-permute-start(bf16[256,4,128]{2,0,1:T(8,128)(2,1)S(1)} %get-tuple-element.439), channel_id=1, source_target_pairs={{0,4},{4,8},{8,12},{12,16},{16,20},{20,24},{24,28},{28,32},{32,36}... | collective-permute-start | bytes 786440 | tf_op jit(solution)/shard_map/while/body/eval_jaxpr/ppermute | solution.py:17
  138.8 10.8 %collective-permute-start.2 = (bf16[256,4,128]{2,0,1:T(8,128)(2,1)}, bf16[256,4,128]{2,0,1:T(8,128)(2,1)}, u32[]{:S(2)}, u32[]{:S(2)}) collective-permute-start(bf16[256,4,128]{2,0,1:T(8,128)(2,1)} %get-tuple-element.440), channel_id=1, source_target_pairs={{0,4},{4,8},{8,12},{12,16},{16,20},{20,24},{24,28},{28,32},{32,36}... | collective-permute-start | bytes 786440 | tf_op jit(solution)/shard_map/while/body/eval_jaxpr/ppermute | solution.py:17
  146.7 10.0 %collective-permute-start.1 = (bf16[256,4,128]{2,0,1:T(8,128)(2,1)}, bf16[256,4,128]{2,0,1:T(8,128)(2,1)S(1)}, u32[]{:S(2)}, u32[]{:S(2)}) collective-permute-start(bf16[256,4,128]{2,0,1:T(8,128)(2,1)} %collective-permute-done), channel_id=1, source_target_pairs={{0,4},{4,8},{8,12},{12,16},{16,20},{20,24},{24,28},{28,32},{32,36}... | collective-permute-start | bytes 786440 | tf_op jit(solution)/shard_map/while/body/eval_jaxpr/ppermute | solution.py:17
  149.6 10.0 %collective-permute-start.3 = (bf16[256,4,128]{2,0,1:T(8,128)(2,1)}, bf16[256,4,128]{2,0,1:T(8,128)(2,1)S(1)}, u32[]{:S(2)}, u32[]{:S(2)}) collective-permute-start(bf16[256,4,128]{2,0,1:T(8,128)(2,1)} %collective-permute-done.2), channel_id=1, source_target_pairs={{0,4},{4,8},{8,12},{12,16},{16,20},{20,24},{24,28},{28,32},{32,36}... | collective-permute-start | bytes 786440 | tf_op jit(solution)/shard_map/while/body/eval_jaxpr/ppermute | solution.py:17
  159.6 2.8 copy-start.7
  163.4 9.9 %collective-permute-start = (bf16[256,4,128]{2,0,1:T(8,128)(2,1)S(1)}, bf16[256,4,128]{2,0,1:T(8,128)(2,1)}, u32[]{:S(2)}, u32[]{:S(2)}) collective-permute-start(bf16[256,4,128]{2,0,1:T(8,128)(2,1)S(1)} %get-tuple-element.439), channel_id=1, source_target_pairs={{0,4},{4,8},{8,12},{12,16},{16,20},{20,24},{24,28},{28,32},{32,36}... | collective-permute-start | bytes 786440 | tf_op jit(solution)/shard_map/while/body/eval_jaxpr/ppermute | solution.py:17
  165.3 10.8 %collective-permute-start.2 = (bf16[256,4,128]{2,0,1:T(8,128)(2,1)}, bf16[256,4,128]{2,0,1:T(8,128)(2,1)}, u32[]{:S(2)}, u32[]{:S(2)}) collective-permute-start(bf16[256,4,128]{2,0,1:T(8,128)(2,1)} %get-tuple-element.440), channel_id=1, source_target_pairs={{0,4},{4,8},{8,12},{12,16},{16,20},{20,24},{24,28},{28,32},{32,36}... | collective-permute-start | bytes 786440 | tf_op jit(solution)/shard_map/while/body/eval_jaxpr/ppermute | solution.py:17
  173.3 10.0 %collective-permute-start.1 = (bf16[256,4,128]{2,0,1:T(8,128)(2,1)}, bf16[256,4,128]{2,0,1:T(8,128)(2,1)S(1)}, u32[]{:S(2)}, u32[]{:S(2)}) collective-permute-start(bf16[256,4,128]{2,0,1:T(8,128)(2,1)} %collective-permute-done), channel_id=1, source_target_pairs={{0,4},{4,8},{8,12},{12,16},{16,20},{20,24},{24,28},{28,32},{32,36}... | collective-permute-start | bytes 786440 | tf_op jit(solution)/shard_map/while/body/eval_jaxpr/ppermute | solution.py:17
  176.1 10.0 %collective-permute-start.3 = (bf16[256,4,128]{2,0,1:T(8,128)(2,1)}, bf16[256,4,128]{2,0,1:T(8,128)(2,1)S(1)}, u32[]{:S(2)}, u32[]{:S(2)}) collective-permute-start(bf16[256,4,128]{2,0,1:T(8,128)(2,1)} %collective-permute-done.2), channel_id=1, source_target_pairs={{0,4},{4,8},{8,12},{12,16},{16,20},{20,24},{24,28},{28,32},{32,36}... | collective-permute-start | bytes 786440 | tf_op jit(solution)/shard_map/while/body/eval_jaxpr/ppermute | solution.py:17
  186.1 2.8 copy-start.7
  189.9 9.9 %collective-permute-start = (bf16[256,4,128]{2,0,1:T(8,128)(2,1)S(1)}, bf16[256,4,128]{2,0,1:T(8,128)(2,1)}, u32[]{:S(2)}, u32[]{:S(2)}) collective-permute-start(bf16[256,4,128]{2,0,1:T(8,128)(2,1)S(1)} %get-tuple-element.439), channel_id=1, source_target_pairs={{0,4},{4,8},{8,12},{12,16},{16,20},{20,24},{24,28},{28,32},{32,36}... | collective-permute-start | bytes 786440 | tf_op jit(solution)/shard_map/while/body/eval_jaxpr/ppermute | solution.py:17
  191.8 10.8 %collective-permute-start.2 = (bf16[256,4,128]{2,0,1:T(8,128)(2,1)}, bf16[256,4,128]{2,0,1:T(8,128)(2,1)}, u32[]{:S(2)}, u32[]{:S(2)}) collective-permute-start(bf16[256,4,128]{2,0,1:T(8,128)(2,1)} %get-tuple-element.440), channel_id=1, source_target_pairs={{0,4},{4,8},{8,12},{12,16},{16,20},{20,24},{24,28},{28,32},{32,36}... | collective-permute-start | bytes 786440 | tf_op jit(solution)/shard_map/while/body/eval_jaxpr/ppermute | solution.py:17
  199.8 10.0 %collective-permute-start.1 = (bf16[256,4,128]{2,0,1:T(8,128)(2,1)}, bf16[256,4,128]{2,0,1:T(8,128)(2,1)S(1)}, u32[]{:S(2)}, u32[]{:S(2)}) collective-permute-start(bf16[256,4,128]{2,0,1:T(8,128)(2,1)} %collective-permute-done), channel_id=1, source_target_pairs={{0,4},{4,8},{8,12},{12,16},{16,20},{20,24},{24,28},{28,32},{32,36}... | collective-permute-start | bytes 786440 | tf_op jit(solution)/shard_map/while/body/eval_jaxpr/ppermute | solution.py:17
  202.6 10.0 %collective-permute-start.3 = (bf16[256,4,128]{2,0,1:T(8,128)(2,1)}, bf16[256,4,128]{2,0,1:T(8,128)(2,1)S(1)}, u32[]{:S(2)}, u32[]{:S(2)}) collective-permute-start(bf16[256,4,128]{2,0,1:T(8,128)(2,1)} %collective-permute-done.2), channel_id=1, source_target_pairs={{0,4},{4,8},{8,12},{12,16},{16,20},{20,24},{24,28},{28,32},{32,36}... | collective-permute-start | bytes 786440 | tf_op jit(solution)/shard_map/while/body/eval_jaxpr/ppermute | solution.py:17
  216.4 9.9 %collective-permute-start = (bf16[256,4,128]{2,0,1:T(8,128)(2,1)S(1)}, bf16[256,4,128]{2,0,1:T(8,128)(2,1)}, u32[]{:S(2)}, u32[]{:S(2)}) collective-permute-start(bf16[256,4,128]{2,0,1:T(8,128)(2,1)S(1)} %get-tuple-element.439), channel_id=1, source_target_pairs={{0,4},{4,8},{8,12},{12,16},{16,20},{20,24},{24,28},{28,32},{32,36}... | collective-permute-start | bytes 786440 | tf_op jit(solution)/shard_map/while/body/eval_jaxpr/ppermute | solution.py:17
  218.3 10.8 %collective-permute-start.2 = (bf16[256,4,128]{2,0,1:T(8,128)(2,1)}, bf16[256,4,128]{2,0,1:T(8,128)(2,1)}, u32[]{:S(2)}, u32[]{:S(2)}) collective-permute-start(bf16[256,4,128]{2,0,1:T(8,128)(2,1)} %get-tuple-element.440), channel_id=1, source_target_pairs={{0,4},{4,8},{8,12},{12,16},{16,20},{20,24},{24,28},{28,32},{32,36}... | collective-permute-start | bytes 786440 | tf_op jit(solution)/shard_map/while/body/eval_jaxpr/ppermute | solution.py:17
  226.3 10.0 %collective-permute-start.1 = (bf16[256,4,128]{2,0,1:T(8,128)(2,1)}, bf16[256,4,128]{2,0,1:T(8,128)(2,1)S(1)}, u32[]{:S(2)}, u32[]{:S(2)}) collective-permute-start(bf16[256,4,128]{2,0,1:T(8,128)(2,1)} %collective-permute-done), channel_id=1, source_target_pairs={{0,4},{4,8},{8,12},{12,16},{16,20},{20,24},{24,28},{28,32},{32,36}... | collective-permute-start | bytes 786440 | tf_op jit(solution)/shard_map/while/body/eval_jaxpr/ppermute | solution.py:17
  229.1 10.0 %collective-permute-start.3 = (bf16[256,4,128]{2,0,1:T(8,128)(2,1)}, bf16[256,4,128]{2,0,1:T(8,128)(2,1)S(1)}, u32[]{:S(2)}, u32[]{:S(2)}) collective-permute-start(bf16[256,4,128]{2,0,1:T(8,128)(2,1)} %collective-permute-done.2), channel_id=1, source_target_pairs={{0,4},{4,8},{8,12},{12,16},{16,20},{20,24},{24,28},{28,32},{32,36}... | collective-permute-start | bytes 786440 | tf_op jit(solution)/shard_map/while/body/eval_jaxpr/ppermute | solution.py:17
  247.6 6.4 copy-start.10
  247.6 6.7 %copy-start.12 = (s32[64]{0:T(128)S(1)}, s32[64]{0:T(128)}, u32[]{:S(2)}) copy-start(s32[64]{0:T(128)} %param.26) | copy-start | bytes 772
  252.3 75.5 %copy-start.9 = (f32[2048]{0:T(1024)S(1)}, f32[2048]{0:T(1024)}, u32[]{:S(2)}) copy-start(f32[2048]{0:T(1024)} %param.23) | copy-start | bytes 24580
  324.4 3.4 copy-start.2
  324.4 3.4 copy-start.3
  584.6 5.2 copy-start.11
  584.6 37.1 %all-to-all-start.2 = ((bf16[4,1,64,10,512]{4,2,3,1,0:T(8,128)(2,1)}), bf16[4,1,64,10,512]{4,2,3,1,0:T(8,128)(2,1)}, u32[]{:S(2)}, u32[]{:S(2)}) async-start(bf16[4,1,64,10,512]{4,2,3,1,0:T(8,128)(2,1)} %copy.100), calls=%async_computation.2 | async-start | bytes 5242880 | tf_op jit(solution)/shard_map/all_to_all | solution.py:153
  (21 other events, 31.7 us)
Sparse Core Ops, SparseCore 0:
  10.1 83.0 all-gather.1
  252.4 71.9 all-reduce.1
